TPU v7x, 256 devices: a whole 4x4x8 slice. The times are simulated.
256 devices in a mesh: gr: 16 (over z, core), gc: 16 (over x, y).
Axes of the slice: x: 4, y: 4, z: 8, core: 2. Of those that a mesh axis runs over, the one named last changes fastest.
Arguments:
- out_grad: bfloat16 [131072, 512], P(('gr', 'gc')), may hold values from -6 to 6
- preactivation_state: bfloat16 [131072, 512], P(('gr', 'gc')), may hold values from -6 to 6
- features: bfloat16 [131072, 512], P(('gc', 'gr')), may hold values from -24 to 24
- weight: bfloat16 [512, 512], replicated, may hold values from -0.25 to 0.25
- block_values: bfloat16 [16, 16, 152, 128, 128], P('gr', 'gc'), may hold values from -0.1875 to 0.1875
- block_rows: int32 [16, 16, 152], P('gr', 'gc'), may hold values from 0 to 63, as said below
- block_cols: int32 [16, 16, 152], P('gr', 'gc'), may hold values from 0 to 63, as said below
- block_counts: int32 [16, 16], P('gr', 'gc'), may hold values from 1 to 152, as said below
Outputs:
- input_grad: bfloat16 [131072, 512], P(('gc', 'gr'))
- weight_grad: float32 [512, 512], replicated
Inputs may be any that keep to these rules, and one draw needn't show every extreme that they name: `block_rows`: block row within a tile; some entry equals 63. `block_cols`: block column within a tile; some entry equals 63. `block_counts`: slots from this count on are unused; some tile uses all 152 slots.
All inputs are finite; a program needn't handle non-finite values.
Results may differ from a plain program's by a relative error of at most 0.014.
Values may be sent and summed in bfloat16 or wider, within the bound.
A program may use at most 128 MiB of HBM per device.

v0:
```python
import math
import jax
import jax.numpy as jnp
from jax import lax
from jax.sharding import PartitionSpec as P


def local(
    out_grad,
    preactivation_state,
    features,
    weight,
    block_values,
    block_rows,
    block_cols,
    block_counts,
):
    masked = jnp.where(preactivation_state > 0, out_grad, jnp.zeros_like(out_grad))
    tile_grads = lax.all_gather(masked, "gc", axis=0, tiled=True)
    block_size = block_values.shape[-1]
    feature_width = masked.shape[1]
    stacked = tile_grads.reshape(-1, block_size, feature_width)
    values_here = block_values[0, 0]
    rows_here = block_rows[0, 0]
    cols_here = block_cols[0, 0]
    count_here = block_counts[0, 0]
    capacity = values_here.shape[0]
    group_size = math.gcd(capacity, 16)
    node_rows = features.shape[0]
    col_count = node_rows * lax.axis_size("gr") // block_size

    def summing_group(current_index, value_partial_sum):
        offset = current_index * group_size
        current_values = lax.dynamic_slice_in_dim(values_here, offset, group_size, 0)
        rows_now = lax.dynamic_slice_in_dim(rows_here, offset, group_size, 0)
        cols_now = lax.dynamic_slice_in_dim(cols_here, offset, group_size, 0)
        selected_entries = stacked[rows_now]
        contribution = jnp.einsum(
            "yql,yqa->yla", current_values, selected_entries, preferred_element_type=jnp.float32
        )
        active = offset + jnp.arange(group_size) < count_here
        contribution = jnp.where(active[:, None, None], contribution, jnp.zeros_like(contribution))
        return value_partial_sum.at[cols_now].add(contribution)

    value_partial_sum = lax.fori_loop(
        0,
        capacity // group_size,
        summing_group,
        jnp.zeros((col_count, block_size, feature_width), jnp.float32),
    )
    value_partial_sum = value_partial_sum.reshape(-1, feature_width)
    column_total = lax.psum(value_partial_sum.astype(jnp.bfloat16), "gr").astype(jnp.float32)
    mine = lax.dynamic_slice_in_dim(column_total, lax.axis_index("gr") * node_rows, node_rows, 0)
    spread = mine.astype(jnp.bfloat16)
    input_grad = lax.dot_general(
        spread, weight, (((1,), (1,)), ((), ())), preferred_element_type=jnp.float32
    ).astype(jnp.bfloat16)
    weight_term = lax.dot_general(
        features, spread, (((0,), (0,)), ((), ())), preferred_element_type=jnp.float32
    )
    scale_factor = (node_rows * lax.axis_size("gr") * lax.axis_size("gc")) ** (-0.5)
    weight_grad = lax.psum(weight_term, ("gr", "gc")) * scale_factor
    return (input_grad, weight_grad)


def solution(mesh):
    in_specs = (
        P(("gr", "gc"), None),
        P(("gr", "gc"), None),
        P(("gc", "gr"), None),
        P(),
        P("gr", "gc", None, None, None),
        P("gr", "gc", None),
        P("gr", "gc", None),
        P("gr", "gc"),
    )
    out_specs = (P(("gc", "gr"), None), P())
    return jax.shard_map(local, mesh=mesh, in_specs=in_specs, out_specs=out_specs, check_vma=False)
```

profile of v0, /device:TPU:2, one launch (start us, length us, event | category | flops | bytes accessed | tf_op | source)
XLA Modules:
  0.0 739.5 jit_solution(15906717005274415228)
XLA Ops:
  7.2 2.1 compare_select_fusion.2
  9.4 7.7 %copy.10 = bf16[1,1,152,128,128]{3,4,2,1,0:T(8,128)(2,1)} copy(bf16[1,1,152,128,128]{4,3,2,1,0:T(8,128)(2,1)} %param.14) | data formatting | bytes 9961472 | tf_op args[4]
  17.1 72.7 %all-gather.2.cloned.1.call-done = bf16[8192,512]{1,0:T(8,128)(2,1)} async-done(((bf16[512,512]{1,0:T(8,128)(2,1)}), bf16[8192,512]{1,0:T(8,128)(2,1)}) %all-gather.2.cloned.1.call-update) | async-done | bytes 8388624 | tf_op jit(solution)/shard_map/all_gather | solution.py:19
  89.8 7.9 %broadcast_in_dim.38 = f32[64,128,512]{2,1,0:T(8,128)} broadcast(f32[]{:T(128)} %constant.51.clone.1), dimensions={} | broadcast | bytes 16777220 | tf_op jit(solution)/shard_map/broadcast_in_dim | solution.py:49
  97.7 224.4 %while.13 = (s32[]{:T(128)}, f32[64,128,512]{2,1,0:T(8,128)}, s32[152]{0:T(256)S(1)}, s32[]{:T(128)}, bf16[152,128,128]{1,2,0:T(8,128)(2,1)}, /*index=5*/s32[152...) while((s32[]{:T(128)}, f32[64,128,512]{2,1,0:T(8,128)}, ...), condition=%wide.region_2.3_spmd, body=%wide.region_0.2_spmd.sunk | while | flops 135267392 | bytes 11800995 | solution.py:45
  97.8 5.0 gather_fusion
  103.4 1.7 convolution_select_fusion.2
  105.1 4.4 scatter_fusion
  109.6 5.0 gather_fusion
  115.2 1.7 convolution_select_fusion.2
  116.9 4.4 scatter_fusion
  121.4 5.0 gather_fusion
  128.8 4.4 scatter_fusion
  133.3 5.0 gather_fusion
  138.9 1.7 convolution_select_fusion.2
  140.7 4.2 scatter_fusion
  145.0 5.0 gather_fusion
  150.6 1.7 convolution_select_fusion.2
  152.3 4.4 scatter_fusion
  156.8 5.0 gather_fusion
  162.4 1.7 convolution_select_fusion.2
  164.2 4.4 scatter_fusion
  168.6 5.0 gather_fusion
  174.3 1.7 convolution_select_fusion.2
  176.0 4.4 scatter_fusion
  180.5 5.0 gather_fusion
  186.1 1.7 convolution_select_fusion.2
  187.8 4.4 scatter_fusion
  192.3 5.0 gather_fusion
  197.9 1.7 convolution_select_fusion.2
  199.7 4.3 scatter_fusion
  204.0 5.0 gather_fusion
  209.6 1.7 convolution_select_fusion.2
  211.4 4.4 scatter_fusion
  215.8 5.0 gather_fusion
  221.4 1.7 convolution_select_fusion.2
  223.2 4.4 scatter_fusion
  227.6 5.0 gather_fusion
  233.2 1.7 convolution_select_fusion.2
  235.0 4.3 scatter_fusion
  239.3 5.0 gather_fusion
  245.0 1.7 convolution_select_fusion.2
  246.7 4.3 scatter_fusion
  251.1 5.0 gather_fusion
  258.5 4.3 scatter_fusion
  262.9 5.0 gather_fusion
  268.5 1.7 convolution_select_fusion.2
  270.3 4.4 scatter_fusion
  274.7 5.0 gather_fusion
  280.3 1.7 convolution_select_fusion.2
  282.1 4.4 scatter_fusion
  286.6 5.0 gather_fusion
  292.2 1.7 convolution_select_fusion.2
  293.9 4.4 scatter_fusion
  298.4 5.0 gather_fusion
  305.8 4.4 scatter_fusion
  310.3 5.0 gather_fusion
  315.9 1.7 convolution_select_fusion.2
  317.6 4.4 scatter_fusion
  322.1 9.0 %convert_element_type.15 = bf16[64,128,512]{2,1,0:T(8,128)(2,1)} convert(f32[64,128,512]{2,1,0:T(8,128)} %get-tuple-element.126) | non-fusion elementwise | flops 4194304 | bytes 25165824 | tf_op jit(solution)/shard_map/convert_element_type | solution.py:52
  331.2 134.8 %all-reduce.3.cloned.1.call-done = bf16[8192,512]{1,0:T(8,128)(2,1)} async-done(((bf16[8192,512]{1,0:T(8,128)(2,1)}), bf16[8192,512]{1,0:T(8,128)(2,1)}) %all-reduce.3.cloned.1.call-update) | async-done | bytes 8388624 | tf_op jit(solution)/shard_map/psum | solution.py:52
  466.0 2.5 convolution_bitcast_fusion
  468.5 2.3 convolution_convert_fusion
  470.8 259.5 %all-reduce.5.cloned.1.call-done = f32[512,512]{0,1:T(8,128)} async-done(((f32[512,512]{0,1:T(8,128)}), f32[512,512]{0,1:T(8,128)}) %all-reduce.5.cloned.1.call-update) | async-done | bytes 1048592 | tf_op jit(solution)/shard_map/psum | solution.py:62
  (76 shorter events, 21.9 us)
Async XLA Ops:
  7.2 458.8 %copy-start = (bf16[512,512]{1,0:T(8,128)(2,1)S(1)}, bf16[512,512]{1,0:T(8,128)(2,1)}, u32[]{:S(2)}) copy-start(bf16[512,512]{1,0:T(8,128)(2,1)} %param.12) | copy-start | bytes 1572868
  7.2 82.6 %all-gather.2.cloned.1.call-start = ((), (), s32[]{:S(2)}) async-start(), calls=%async_computation | async-start | bytes 8912896 | tf_op jit(solution)/shard_map/all_gather | solution.py:19
  9.3 456.6 %all-reduce.3.cloned.1.call-start = ((), (), s32[]{:S(2)}) async-start(), calls=%async_computation.1 | async-start | bytes 16777216 | tf_op jit(solution)/shard_map/psum | solution.py:52
  89.8 7.9 %copy-start.2 = (s32[1,1,152]{2,1,0:T(1,128)S(1)}, s32[1,1,152]{2,1,0:T(1,128)}, u32[]{:S(2)}) copy-start(s32[1,1,152]{2,1,0:T(1,128)} %param.16) | copy-start | bytes 1828
  89.8 7.9 %copy-start.3 = (s32[1,1,152]{2,1,0:T(1,128)S(1)}, s32[1,1,152]{2,1,0:T(1,128)}, u32[]{:S(2)}) copy-start(s32[1,1,152]{2,1,0:T(1,128)} %param.15) | copy-start | bytes 1828
  331.1 137.4 %copy-start.1 = (bf16[512,512]{1,0:T(8,128)(2,1)S(1)}, bf16[512,512]{1,0:T(8,128)(2,1)}, u32[]{:S(2)}) copy-start(bf16[512,512]{1,0:T(8,128)(2,1)} %param.13) | copy-start | bytes 1572868
  331.1 399.2 %all-reduce.5.cloned.1.call-start = ((), (), s32[]{:S(2)}) async-start(), calls=%async_computation.2 | async-start | bytes 2097152 | tf_op jit(solution)/shard_map/psum | solution.py:62
Sparse Core Ops, SparseCore 0:
  11.0 78.7 all-gather.1
  331.2 134.7 all-reduce.2
  472.0 258.2 all-reduce.4
where the time goes:
time: 742 us; the launch traced here: 739 us
  waiting for transfers between devices  467 us (63%)
  local copies, waits for them, and re-layouts  111 us (15%)
  other arithmetic  109 us (15%)
  matrix products  37.8 us (5%)
  between operations  13.8 us (2%)
    psum x1, waiting for transfers between devices, local(): weight_grad = lax.psum(weight_term, ('gr', 'gc')) * scale_factor  260 us
    psum x1, waiting for transfers between devices, local(): lax.psum(value_partial_sum.astype(jnp.bfloat16), 'gr').astype(jnp.float32)  135 us
    gather x19, local copies, waits for them, and re-layouts, summing_group(): selected_entries = stacked[rows_now]  94.3 us
    scatter-add x19, other arithmetic, summing_group(): return value_partial_sum.at[cols_now].add(contribution)  82.9 us
    all_gather x1, waiting for transfers between devices, local(): tile_grads = lax.all_gather(masked, 'gc', axis=0, tiled=True)  72.7 us
    dot_general x19, matrix products, summing_group(): jnp.einsum('yql,yqa->yla', current_values, selected_entries, preferred_el...  33 us
  transfers between devices with their start and end apart: 3, of which 3 were waited for; matrix products, arithmetic and copies ran while one was open for 1% of the time, Pallas kernels for 0%

commit v1 on v0

--- a/solution.py
+++ b/solution.py
@@ -16,7 +16,8 @@
     block_counts,
 ):
     masked = jnp.where(preactivation_state > 0, out_grad, jnp.zeros_like(out_grad))
-    tile_grads = lax.all_gather(masked, "gc", axis=0, tiled=True)
+    sent = jnp.stack([masked] * lax.axis_size("gc"))
+    tile_grads = jnp.concatenate(lax.all_to_all(sent, "gc", 0, 0), axis=0)
     block_size = block_values.shape[-1]
     feature_width = masked.shape[1]
     stacked = tile_grads.reshape(-1, block_size, feature_width)

time: 742 us -> 825 us (1.11)
  waiting for transfers between devices: 467 us -> 539 us
    all_to_all x0 -> x1, waiting for transfers between devices: none -> 97.1 us  [local(): tile_grads = jnp.concatenate(lax.all_to_all(sent, 'gc', 0, 0), axis=0)]
    all_gather x1 -> x0, waiting for transfers between devices: 72.7 us -> none  [local(): tile_grads = lax.all_gather(masked, 'gc', axis=0, tiled=True)]
    psum x1, waiting for transfers between devices: 135 us -> 182 us  [local(): lax.psum(value_partial_sum.astype(jnp.bfloat16), 'gr').astype(jnp.float32)]
where the time goes in v1:
time: 825 us; the launch traced here: 822 us
  waiting for transfers between devices  539 us (65%)
  local copies, waits for them, and re-layouts  115 us (14%)
  other arithmetic  108 us (13%)
  matrix products  37.8 us (5%)
  between operations  14.1 us (2%)
    psum x1, waiting for transfers between devices, local(): weight_grad = lax.psum(weight_term, ('gr', 'gc')) * scale_factor  259 us
    psum x1, waiting for transfers between devices, local(): lax.psum(value_partial_sum.astype(jnp.bfloat16), 'gr').astype(jnp.float32)  182 us
    all_to_all x1, waiting for transfers between devices, local(): tile_grads = jnp.concatenate(lax.all_to_all(sent, 'gc', 0, 0), axis=0)  97.1 us
    gather x19, local copies, waits for them, and re-layouts, summing_group(): selected_entries = stacked[rows_now]  94.3 us
    scatter-add x19, other arithmetic, summing_group(): return value_partial_sum.at[cols_now].add(contribution)  82.8 us
    dot_general x19, matrix products, summing_group(): jnp.einsum('yql,yqa->yla', current_values, selected_entries, preferred_el...  33 us
  transfers between devices with their start and end apart: 3, of which 3 were waited for; matrix products, arithmetic and copies ran while one was open for 1% of the time, Pallas kernels for 0%

profile of v1, /device:TPU:2, one launch (start us, length us, event | category | flops | bytes accessed | tf_op | source)
XLA Modules:
  0.0 822.1 jit_solution(1646732010114654779)
XLA Ops:
  8.5 4.0 stack.2
  12.5 7.5 all-to-all-start
  20.1 7.6 copy.10
  27.7 97.1 %all-to-all-done = bf16[16,512,512]{2,1,0:T(8,128)(2,1)} async-done(((bf16[16,512,512]{2,1,0:T(8,128)(2,1)}), bf16[16,512,512]{2,1,0:T(8,128)(2,1)}, u32[]{:S(2)}, u32[]{:S(2)}) %all-to-all-start) | async-done | bytes 8388640 | tf_op jit(solution)/shard_map/all_to_all | solution.py:20
  124.8 7.9 broadcast_in_dim.38
  132.7 224.3 %while.13 = (s32[]{:T(128)}, f32[64,128,512]{2,1,0:T(8,128)}, s32[152]{0:T(256)S(1)}, s32[]{:T(128)}, bf16[152,128,128]{1,2,0:T(8,128)(2,1)}, /*index=5*/s32[152...) while((s32[]{:T(128)}, f32[64,128,512]{2,1,0:T(8,128)}, ...), condition=%wide.region_2.3_spmd, body=%wide.region_0.2_spmd.sunk | while | flops 135267392 | bytes 11800995 | solution.py:46
  132.8 5.0 gather_fusion
  138.4 1.7 convolution_select_fusion.2
  140.2 4.3 scatter_fusion
  144.6 5.0 gather_fusion
  150.2 1.7 convolution_select_fusion.2
  151.9 4.4 scatter_fusion
  156.4 5.0 gather_fusion
  162.0 1.7 convolution_select_fusion.2
  163.8 4.4 scatter_fusion
  168.2 5.0 gather_fusion
  173.9 1.7 convolution_select_fusion.2
  175.6 4.2 scatter_fusion
  179.9 5.0 gather_fusion
  185.5 1.7 convolution_select_fusion.2
  187.2 4.4 scatter_fusion
  191.7 5.0 gather_fusion
  197.4 1.7 convolution_select_fusion.2
  199.1 4.4 scatter_fusion
  203.6 5.0 gather_fusion
  209.2 1.7 convolution_select_fusion.2
  210.9 4.4 scatter_fusion
  215.4 5.0 gather_fusion
  221.0 1.7 convolution_select_fusion.2
  222.8 4.4 scatter_fusion
  227.2 5.0 gather_fusion
  232.8 1.7 convolution_select_fusion.2
  234.6 4.3 scatter_fusion
  239.0 5.0 gather_fusion
  244.6 1.7 convolution_select_fusion.2
  246.3 4.4 scatter_fusion
  250.8 5.0 gather_fusion
  258.1 4.3 scatter_fusion
  262.6 5.0 gather_fusion
  268.2 1.7 convolution_select_fusion.2
  269.9 4.3 scatter_fusion
  274.3 5.0 gather_fusion
  279.9 1.7 convolution_select_fusion.2
  281.7 4.3 scatter_fusion
  286.1 5.0 gather_fusion
  291.7 1.7 convolution_select_fusion.2
  293.4 4.3 scatter_fusion
  297.9 5.0 gather_fusion
  303.5 1.7 convolution_select_fusion.2
  305.2 4.4 scatter_fusion
  309.7 5.0 gather_fusion
  315.3 1.7 convolution_select_fusion.2
  317.0 4.4 scatter_fusion
  321.5 5.0 gather_fusion
  328.9 4.4 scatter_fusion
  333.4 5.0 gather_fusion
  340.7 4.4 scatter_fusion
  345.2 5.0 gather_fusion
  352.5 4.4 scatter_fusion
  357.0 9.0 %convert_element_type.15 = bf16[64,128,512]{2,1,0:T(8,128)(2,1)} convert(f32[64,128,512]{2,1,0:T(8,128)} %get-tuple-element.126) | non-fusion elementwise | flops 4194304 | bytes 25165824 | tf_op jit(solution)/shard_map/convert_element_type | solution.py:53
  366.1 182.3 %all-reduce.3.cloned.1.call-done = bf16[8192,512]{1,0:T(8,128)(2,1)} async-done(((bf16[8192,512]{1,0:T(8,128)(2,1)}), bf16[8192,512]{1,0:T(8,128)(2,1)}) %all-reduce.3.cloned.1.call-update) | async-done | bytes 8388624 | tf_op jit(solution)/shard_map/psum | solution.py:53
  548.4 2.5 convolution_bitcast_fusion
  550.9 2.3 convolution_convert_fusion
  553.2 259.4 %all-reduce.5.cloned.1.call-done = f32[512,512]{0,1:T(8,128)} async-done(((f32[512,512]{0,1:T(8,128)}), f32[512,512]{0,1:T(8,128)}) %all-reduce.5.cloned.1.call-update) | async-done | bytes 1048592 | tf_op jit(solution)/shard_map/psum | solution.py:63
  (76 shorter events, 24.9 us)
Async XLA Ops:
  7.2 541.2 %copy-start = (bf16[512,512]{1,0:T(8,128)(2,1)S(1)}, bf16[512,512]{1,0:T(8,128)(2,1)}, u32[]{:S(2)}) copy-start(bf16[512,512]{1,0:T(8,128)(2,1)} %param.12) | copy-start | bytes 1572868
  12.5 112.3 %all-to-all-start = ((bf16[16,512,512]{2,1,0:T(8,128)(2,1)}), bf16[16,512,512]{2,1,0:T(8,128)(2,1)}, u32[]{:S(2)}, u32[]{:S(2)}) async-start(bf16[16,512,512]{2,1,0:T(8,128)(2,1)} %stack.2), calls=%async_computation | async-start | bytes 16777216 | tf_op jit(solution)/shard_map/all_to_all | solution.py:20
  20.0 528.3 %all-reduce.3.cloned.1.call-start = ((), (), s32[]{:S(2)}) async-start(), calls=%async_computation.1 | async-start | bytes 16777216 | tf_op jit(solution)/shard_map/psum | solution.py:53
  124.8 7.9 copy-start.2
  124.8 7.9 copy-start.3
  366.0 184.9 %copy-start.1 = (bf16[512,512]{1,0:T(8,128)(2,1)S(1)}, bf16[512,512]{1,0:T(8,128)(2,1)}, u32[]{:S(2)}) copy-start(bf16[512,512]{1,0:T(8,128)(2,1)} %param.13) | copy-start | bytes 1572868
  366.0 446.6 %all-reduce.5.cloned.1.call-start = ((), (), s32[]{:S(2)}) async-start(), calls=%async_computation.2 | async-start | bytes 2097152 | tf_op jit(solution)/shard_map/psum | solution.py:63
Sparse Core Ops, SparseCore 0:
  366.2 182.1 all-reduce.2
  554.4 258.2 all-reduce.4
